TPU v7x, 32 devices: a whole 2x2x4 slice. The times are simulated.
32 devices in a mesh: fields: 2 (over x), vel: 8 (over z, y), rows: 2 (over core).
Axes of the slice: x: 2, y: 2, z: 4, core: 2. Of those that a mesh axis runs over, the one named last changes fastest.
Arguments:
- images: float32 [16, 64, 4096], P(('fields', 'vel'), 'rows'), parts along dimension 0, may hold values from -6 to 6
- variance: float32 [16, 64, 4096], P(('fields', 'vel'), 'rows'), parts along dimension 0, may hold values from 0.5 to 2
- spread_kernel: float32 [21, 21], replicated, may hold values from 0.05 to 1
- shifts: int32 [576, 3, 2], P(('fields', 'vel')), parts along dimension 0, may hold values from -16 to 16, as said below
- epoch_owner: int32 [6], P('fields'), parts along dimension 0, may hold values from 0 to 7, as said below
- valid_rows: int32 [6, 2], P('fields'), parts along dimension 0, may hold values from 0 to 64, as said below
Outputs:
- likelihood: float32 [576, 64, 4096], P(('fields', 'vel'), 'rows'), parts along dimension 0
There are 2 independent parts, one for each index of `fields`. A program takes and returns all parts, laid end to end along the dimension named above; an argument that names none is the same for every part. Nothing has to cross between parts.
Inputs may be any that keep to these rules, and one draw needn't show every extreme that they name: `shifts`: each entry lies in -16 to 16; both ends are taken in every draw. `epoch_owner`: the epochs are held by distinct slots. `valid_rows`: in each row the first entry is below the second; the first epoch starts at row 0 and the last ends at row 64.
All inputs are finite; a program needn't handle non-finite values.
Results may differ from a plain program's by a relative error of at most 0.0003.
Values sent between devices are 32-bit elements; how exact they have to be, the bound alone decides.
A program may use at most 128 MiB of HBM per device.

v0:
```python
import jax
import jax.numpy as jnp
from jax import lax
from jax.sharding import PartitionSpec as P

MAXS = 16
EPOCHS = 3


def with_halo(value, sides, width):
    for axis, dim in sides:
        count, length = (lax.axis_size(axis), value.shape[dim])
        up = [(i, (i + 1) % count) for i in range(count - 1)]
        down = [(j, i) for i, j in up]
        last = lax.slice_in_dim(value, length - width, length, axis=dim)
        initial = lax.slice_in_dim(value, 0, width, axis=dim)
        before = lax.ppermute(last, axis, up)
        after = lax.ppermute(initial, axis, down)
        value = jnp.concatenate([before, value, after], axis=dim)
    return value


def spread(value, axis, root):
    mine = lax.axis_index(axis) == root
    return lax.psum(jnp.where(mine, value, jnp.zeros_like(value)), axis)


def band_matrix(kernels, ksize):
    inner = jnp.arange(128 + ksize - 1, dtype=jnp.int32)[:, None, None]
    outer = jnp.arange(128, dtype=jnp.int32)[None, :, None]
    offsets = jnp.arange(ksize, dtype=jnp.int32)[None, None, :]
    onehot = (inner - outer == offsets).astype(jnp.float32)
    return jnp.einsum("fkj,cdj->fkcd", kernels, onehot, precision=lax.Precision.HIGHEST)


def correlate_pair(extended, banded, ksize):
    half = ksize // 2
    height = extended.shape[1] - (ksize - 1)
    columns = extended.shape[2]
    blocks = columns // 128
    padded = jnp.pad(extended, ((0, 0), (0, 0), (half, 128 - half)))

    def add_row(offset, summed):
        row_band = lax.dynamic_slice_in_dim(padded, offset, height, 1)
        leading = row_band[:, :, :columns].reshape(2, height, blocks, 128)
        trailing = row_band[:, :, 128:].reshape(2, height, blocks, 128)[..., : ksize - 1]
        window = jnp.concatenate([leading, trailing], axis=3)
        weights = lax.dynamic_index_in_dim(banded, offset, 1, keepdims=False)
        return summed + jnp.einsum(
            "fhbc,fcd->fhbd", window, weights, precision=lax.Precision.HIGHEST
        )

    summed = lax.fori_loop(0, ksize, add_row, jnp.zeros((2, height, blocks, 128), jnp.float32))
    return summed.reshape(2, height, columns)


def local(images, variance, spread_kernel, shifts, epoch_owner, valid_rows):
    exposure = images[0]
    noise_var = variance[0]
    band_rows = exposure.shape[0]
    columns = exposure.shape[1]
    ksize = spread_kernel.shape[0]
    half = ksize // 2
    kernel_norm = spread_kernel / jnp.sum(spread_kernel)
    kernel_sq = kernel_norm * kernel_norm
    floor = 0.5 * jnp.sum(kernel_sq)
    vel_index = lax.axis_index("vel")
    row_index = lax.axis_index("rows")
    owned = epoch_owner == vel_index
    lower_row = jnp.sum(jnp.where(owned, valid_rows[:, 0], 0))
    upper_row = jnp.sum(jnp.where(owned, valid_rows[:, 1], 0))
    row_ids = row_index * band_rows + jnp.arange(band_rows, dtype=jnp.int32)[:, None]
    usable = (row_ids >= lower_row) & (row_ids < upper_row)
    weighted = jnp.where(usable, exposure / noise_var, jnp.float32(0.0))
    inverse = jnp.where(usable, 1.0 / noise_var, jnp.float32(0.0))
    fields_pair = jnp.stack([weighted, inverse])
    extended = with_halo(fields_pair, (("rows", 1),), half)
    banded = band_matrix(jnp.stack([kernel_norm, kernel_sq]), ksize)
    correlated = correlate_pair(extended, banded, ksize)
    narrow = jnp.stack([spread(correlated, "vel", epoch_owner[epoch]) for epoch in range(EPOCHS)])
    stacked = with_halo(narrow, (("rows", 2),), MAXS)
    padded_all = jnp.pad(stacked, ((0, 0), (0, 0), (0, 0), (128, 128)))

    def one_velocity(shift):
        summed = jnp.zeros((2, band_rows, columns), jnp.float32)
        for epoch in range(EPOCHS):
            start_row = MAXS + shift[epoch, 0]
            start_col = 128 + shift[epoch, 1]
            summed = summed + lax.dynamic_slice(
                padded_all[epoch], (jnp.int32(0), start_row, start_col), (2, band_rows, columns)
            )
        return summed[0] / jnp.sqrt(jnp.maximum(summed[1], floor))

    return lax.map(one_velocity, shifts)


def solution(mesh):
    in_specs = (
        P(("fields", "vel"), "rows", None),
        P(("fields", "vel"), "rows", None),
        P(),
        P(("fields", "vel"), None, None),
        P("fields"),
        P("fields", None),
    )
    out_specs = P(("fields", "vel"), "rows", None)
    return jax.shard_map(local, mesh=mesh, in_specs=in_specs, out_specs=out_specs, check_vma=False)
```

profile of v0, /device:TPU:0, one launch (start us, length us, event | category | flops | bytes accessed | tf_op | source)
XLA Modules:
  0.0 797.7 jit_solution(17309083965974283387)
XLA Ops:
  11.7 2.4 collective-permute-start
  19.9 3.4 fusion.16
  25.3 131.3 %while.28 = (s32[]{:T(128)}, f32[2,32,32,128]{3,2,1,0:T(8,128)S(1)}, f32[2,52,4224]{2,1,0:T(8,128)}, f32[2,21,148,128]{3,1,2,0:T(8,128)}, s32[]{:T(128)}, /*index=5*/s32[]{:T(128)}, s32[]{}) while((s32[]{:T(128)}, f32[2,32,32,128]{3,2,1,0:T(8,128)S(1)}, f32[2,52,4224]{2,1,0:T(8,128)}, f32[2,21,148,128]{3,1,2,0:T(8,128)}, ...), condition=%wide.region_4.5_spmd.clone, body=%wide.region_3.4_spmd.clone.sunk | while | flops 466395136 | bytes 12152943 | solution.py:53
  29.3 2.3 fusion.41
  35.6 2.3 fusion.41
  41.9 2.3 fusion.41
  48.2 2.3 fusion.41
  54.5 2.3 fusion.41
  60.7 2.3 fusion.41
  67.0 2.3 fusion.41
  73.3 2.3 fusion.41
  79.6 2.3 fusion.41
  85.8 2.3 fusion.41
  92.0 2.3 fusion.41
  98.3 2.3 fusion.41
  104.5 2.3 fusion.41
  110.7 2.3 fusion.41
  117.0 2.3 fusion.41
  123.2 2.3 fusion.41
  135.6 2.3 fusion.41
  141.9 2.3 fusion.41
  154.3 2.3 fusion.41
  158.0 2.4 stack.30
  162.8 131.9 %all-reduce.5.cloned.1.call-done = (f32[1,2,32,4096]{3,2,1,0:T(8,128)}, f32[1,2,32,4096]{3,2,1,0:T(8,128)}, f32[1,2,32,4096]{3,2,1,0:T(8,128)}) async-done(((f32[1,2,32,4096]{3,2,1,0:T(8,128)}, f32[1,2,32,4096]{3,2,1,0:T(8,128)}, f32[1,2,32,4096]{3,2,1,0:T(8,128)}), (f32[1,2,32,4096]{3,2,1,0:T(8,128)}, f32[1,2,32,4096]{3,2,1,0:T(8,128)}, f32[1,2,32,4096]{3,2,1,0:T(8,128)})) %all-reduce.5.cloned.1.call-update) | async-done | bytes 3145744 | tf_op jit(solution)/shard_map/psum | solution.py:25
  298.5 2.7 collective-permute-start.2
  303.3 3.5 collective-permute-done.3
  306.8 4.4 select_maximum_fusion
  311.1 479.7 %while.27 = (s32[]{:T(128)}, f32[36,32,4096]{2,1,0:T(8,128)}, f32[3,2,64,4352]{3,2,1,0:T(8,128)}, s32[36,3,2]{1,2,0:T(2,128)S(1)}, f32[]{:T(128)}, /*index=5*/s3...) while((s32[]{:T(128)}, f32[36,32,4096]{2,1,0:T(8,128)}, ...), condition=%wide.region_10.11_spmd, body=%wide.region_9.10_spmd.sunk | while | flops 786458 | bytes 19138044 | solution.py:94
  319.2 3.4 fusion.36
  332.6 3.4 fusion.36
  345.9 3.4 fusion.36
  359.2 3.4 fusion.36
  372.5 3.4 fusion.36
  385.9 3.4 fusion.36
  399.2 3.4 fusion.36
  412.5 3.4 fusion.36
  425.8 3.4 fusion.36
  439.2 3.4 fusion.36
  452.5 3.4 fusion.36
  465.8 3.4 fusion.36
  479.1 3.4 fusion.36
  492.5 3.4 fusion.36
  505.8 3.4 fusion.36
  519.1 3.4 fusion.36
  532.4 3.4 fusion.36
  545.7 3.4 fusion.36
  559.0 3.4 fusion.36
  572.3 3.4 fusion.36
  585.7 3.4 fusion.36
  599.0 3.4 fusion.36
  612.3 3.4 fusion.36
  625.6 3.4 fusion.36
  639.0 3.4 fusion.36
  652.3 3.4 fusion.36
  665.6 3.4 fusion.36
  679.0 3.4 fusion.36
  692.3 3.4 fusion.36
  705.6 3.4 fusion.36
  719.0 3.4 fusion.36
  732.3 3.4 fusion.36
  745.6 3.4 fusion.36
  758.9 3.4 fusion.36
  772.3 3.4 fusion.36
  785.6 3.4 fusion.36
  (266 shorter events, 194.6 us)
Async XLA Ops:
  6.5 10.8 %copy-start.3 = (s32[3]{0:T(128)S(1)}, s32[3]{0:T(128)}, u32[]{:S(2)}) copy-start(s32[3]{0:T(128)} %param.14) | copy-start | bytes 40
  6.5 8.9 %copy-start.2 = (f32[21,21]{1,0:T(8,128)S(1)}, f32[21,21]{1,0:T(8,128)}, u32[]{:S(2)}) copy-start(f32[21,21]{1,0:T(8,128)} %param.12) | copy-start | bytes 5296
  6.5 288.2 %all-reduce.5.cloned.1.call-start = ((), (), s32[]{:S(2)}) async-start(), calls=%async_computation | async-start | bytes 6291456 | tf_op jit(solution)/shard_map/psum | solution.py:25
  11.7 11.7 %collective-permute-start = (f32[2,10,4096]{2,1,0:T(8,128)}, f32[2,10,4096]{2,1,0:T(8,128)S(1)}, u32[]{:S(2)}, u32[]{:S(2)}) collective-permute-start(f32[2,10,4096]{2,1,0:T(8,128)} %get-tuple-element.238), channel_id=1, source_target_pairs={{0,1},{2,3},{4,5},{6,7},{8,9},{10,11},{12,13},{14,15},{16,17},{18,... | collective-permute-start | bytes 983048 | tf_op jit(solution)/shard_map/ppermute | solution.py:17
  14.1 9.2 %collective-permute-start.1 = (f32[2,10,4096]{2,1,0:T(8,128)}, f32[2,10,4096]{2,1,0:T(8,128)S(1)}, u32[]{:S(2)}, u32[]{:S(2)}) collective-permute-start(f32[2,10,4096]{2,1,0:T(8,128)} %get-tuple-element.239), channel_id=1, source_target_pairs={{1,0},{3,2},{5,4},{7,6},{9,8},{11,10},{13,12},{15,14},{17,16},{19,... | collective-permute-start | bytes 983048 | tf_op jit(solution)/shard_map/ppermute | solution.py:18
  294.7 1.5 copy-start.1
  294.7 1.9 copy-start
  296.6 5.8 copy-start.4
  298.5 4.8 collective-permute-start.2
  301.1 5.6 collective-permute-start.3
Sparse Core Ops, SparseCore 0:
  162.9 131.7 all-reduce.4
where the time goes:
time: 803 us; the launch traced here: 798 us
  loops' own time  270 us (34%)
  local copies, waits for them, and re-layouts  238 us (30%)
  waiting for transfers between devices  136 us (17%)
  other arithmetic  79.2 us (10%)
  matrix products  51.7 us (6%)
  between operations  16.1 us (2%)
    another operation x1, loops' own time, local(): return lax.map(one_velocity, shifts)  269 us
    psum x1, waiting for transfers between devices, spread(): return lax.psum(jnp.where(mine, value, jnp.zeros_like(value)), axis)  132 us
    slice x36, local copies, waits for them, and re-layouts, one_velocity(): padded_all[epoch]  123 us
    dot_general x21, matrix products, add_row(): jnp.einsum('fhbc,fcd->fhbd', window, weights, precision=lax.Precision.HIG...  48.3 us
    slice x21, local copies, waits for them, and re-layouts, add_row(): leading = row_band[:, :, :columns].reshape(2, height, blocks, 128)  44.7 us
    add x36, other arithmetic, one_velocity(): summed + lax.dynamic_slice(padded_all[epoch], (jnp.int32(0), start_row, s...  32.9 us
    dynamic_update_slice x36, other arithmetic, local(): return lax.map(one_velocity, shifts)  31.5 us
    dynamic_slice x21, local copies, waits for them, and re-layouts, add_row(): weights = lax.dynamic_index_in_dim(banded, offset, 1, keepdims=False)  29.3 us
  transfers between devices with their start and end apart: 5, of which 3 were waited for; matrix products, arithmetic and copies ran while one was open for 1% of the time, Pallas kernels for 0%

commit v1 on v0

--- a/solution.py
+++ b/solution.py
@@ -1,10 +1,20 @@
+import functools
+
 import jax
 import jax.numpy as jnp
 from jax import lax
+from jax.experimental import pallas as pl
+from jax.experimental.pallas import tpu as pltpu
 from jax.sharding import PartitionSpec as P
 
 MAXS = 16
 EPOCHS = 3
+LANES = 128
+
+
+def spread(value, axis, root):
+    mine = lax.axis_index(axis) == root
+    return lax.psum(jnp.where(mine, value, jnp.zeros_like(value)), axis)
 
 
 def with_halo(value, sides, width):
@@ -18,11 +28,6 @@
         after = lax.ppermute(initial, axis, down)
         value = jnp.concatenate([before, value, after], axis=dim)
     return value
-
-
-def spread(value, axis, root):
-    mine = lax.axis_index(axis) == root
-    return lax.psum(jnp.where(mine, value, jnp.zeros_like(value)), axis)
 
 
 def band_matrix(kernels, ksize):
@@ -54,6 +59,91 @@
     return summed.reshape(2, height, columns)
 
 
+def stack_kernel(bands, band, shift_ref, where_ref, floor_ref, planes_ref, out_ref, held, sem):
+    pieces, count, width, rows, _ = planes_ref.shape
+    vel = pl.program_id(0)
+    blocks = held.shape[1] - 2
+
+    @pl.when(vel == 0)
+    def _():
+        copies = []
+        for p in range(pieces):
+            copies.append(
+                pltpu.make_async_copy(
+                    planes_ref.at[p],
+                    held.at[:, pl.ds(1 + p * width, width), pl.ds(MAXS, rows), :],
+                    sem.at[p],
+                )
+            )
+        for c in copies:
+            c.start()
+        for f in range(count):
+            held[f, 0] = jnp.zeros(held.shape[2:], jnp.float32)
+            held[f, blocks + 1] = jnp.zeros(held.shape[2:], jnp.float32)
+            edge = jnp.zeros((blocks, MAXS, LANES), jnp.float32)
+            held[f, 1 : blocks + 1, 0:MAXS] = edge
+            held[f, 1 : blocks + 1, MAXS + rows : 2 * MAXS + rows] = edge
+        for c in copies:
+            c.wait()
+
+    floor = floor_ref[0]
+    lane = lax.broadcasted_iota(jnp.int32, (band, LANES), 1)
+    first_row = where_ref[0] + MAXS
+    places = []
+    for e in range(EPOCHS):
+        dy = shift_ref[(vel * EPOCHS + e) * 2]
+        dx = shift_ref[(vel * EPOCHS + e) * 2 + 1]
+        back = jnp.where(dx < 0, 1, 0)
+        offset = dx + back * LANES
+        amount = jnp.where(offset == 0, 0, LANES - offset)
+        keep = lane < LANES - offset
+        places.append((first_row + dy, 1 - back, amount, keep))
+
+    def rolled(e, f, b):
+        row, start, amount, _ = places[e]
+        return pltpu.roll(held[2 * e + f, start + b, pl.ds(row, band), :], amount, 1)
+
+    def step(b, before):
+        sums = [None, None]
+        after = []
+        for e in range(EPOCHS):
+            for f in range(2):
+                new = rolled(e, f, b + 1)
+                term = jnp.where(places[e][3], before[2 * e + f], new)
+                after.append(new)
+                sums[f] = term if sums[f] is None else sums[f] + term
+        value = sums[0] * lax.rsqrt(jnp.maximum(sums[1], floor))
+        out_ref[0, :, pl.ds(pl.multiple_of(b * LANES, LANES), LANES)] = value
+        return tuple(after)
+
+    initial = tuple(rolled(e, f, 0) for e in range(EPOCHS) for f in range(2))
+    lax.fori_loop(0, blocks, step, initial, unroll=4)
+
+
+def stack(planes, shifts, floor, band, row_index):
+    pieces, count, width, rows, _ = planes.shape
+    velocities = shifts.shape[0]
+    blocks = pieces * width
+    smem = pl.BlockSpec(memory_space=pltpu.SMEM)
+    return pl.pallas_call(
+        functools.partial(stack_kernel, rows // band, band),
+        grid=(velocities,),
+        out_shape=jax.ShapeDtypeStruct((velocities, band, blocks * LANES), jnp.float32),
+        in_specs=[smem, smem, smem, pl.BlockSpec(memory_space=pl.ANY)],
+        out_specs=pl.BlockSpec((1, band, blocks * LANES), lambda v: (v, 0, 0)),
+        scratch_shapes=[
+            pltpu.VMEM((count, blocks + 2, rows + 2 * MAXS, LANES), jnp.float32),
+            pltpu.SemaphoreType.DMA((pieces,)),
+        ],
+        name="stack",
+    )(
+        shifts.reshape(-1),
+        (row_index * band).astype(jnp.int32).reshape(1),
+        floor.reshape(1),
+        planes,
+    )
+
+
 def local(images, variance, spread_kernel, shifts, epoch_owner, valid_rows):
     exposure = images[0]
     noise_var = variance[0]
@@ -78,20 +168,10 @@
     banded = band_matrix(jnp.stack([kernel_norm, kernel_sq]), ksize)
     correlated = correlate_pair(extended, banded, ksize)
     narrow = jnp.stack([spread(correlated, "vel", epoch_owner[epoch]) for epoch in range(EPOCHS)])
-    stacked = with_halo(narrow, (("rows", 2),), MAXS)
-    padded_all = jnp.pad(stacked, ((0, 0), (0, 0), (0, 0), (128, 128)))
-
-    def one_velocity(shift):
-        summed = jnp.zeros((2, band_rows, columns), jnp.float32)
-        for epoch in range(EPOCHS):
-            start_row = MAXS + shift[epoch, 0]
-            start_col = 128 + shift[epoch, 1]
-            summed = summed + lax.dynamic_slice(
-                padded_all[epoch], (jnp.int32(0), start_row, start_col), (2, band_rows, columns)
-            )
-        return summed[0] / jnp.sqrt(jnp.maximum(summed[1], floor))
-
-    return lax.map(one_velocity, shifts)
+    whole = lax.all_gather(narrow, "rows", axis=2, tiled=True)
+    rows = whole.shape[2]
+    planes = whole.reshape(2 * EPOCHS, rows, columns // LANES, LANES).transpose(0, 2, 1, 3)
+    return stack(planes[None], shifts, floor, band_rows, row_index)
 
 
 def solution(mesh):

time: 803 us -> 356 us (0.44)
  loops' own time: 270 us -> 1.05 us
  local copies, waits for them, and re-layouts: 238 us -> 63.8 us
  other arithmetic: 79.2 us -> 13.4 us
  Pallas kernels: 0 us -> 58.3 us
  waiting for transfers between devices: 136 us -> 146 us
    another operation x1 -> x0, loops' own time: 269 us -> none  [local(): return lax.map(one_velocity, shifts)]
    slice x73 -> x0, local copies, waits for them, and re-layouts: 148 us -> none  [the longest x36 123 us: one_velocity(): padded_all[epoch]]
    pallas_call x0 -> x1, Pallas kernels: none -> 58.3 us  [stack(): pl.pallas_call(functools.partial(stack_kernel, rows // band, band), grid=...]
    slice x21, local copies, waits for them, and re-layouts: 44.7 us -> 7.8 us  [add_row(): leading = row_band[:, :, :columns].reshape(2, height, blocks, 128)]
    add x36 -> x0, other arithmetic: 32.9 us -> none  [one_velocity(): summed + lax.dynamic_slice(padded_all[epoch], (jnp.int32(0), start_row, s...]
    dynamic_update_slice x36 -> x0, other arithmetic: 31.5 us -> none  [local(): return lax.map(one_velocity, shifts)]
    all_gather x0 -> x1, waiting for transfers between devices: none -> 13.8 us  [local(): whole = lax.all_gather(narrow, 'rows', axis=2, tiled=True)]
  transfers between devices with their start and end apart: 5 -> 4, of which waited for: 3 -> 2; matrix products, arithmetic and copies ran while one was open for 1% -> 2% of each run, Pallas kernels for 0% -> 0%
where the time goes in v1:
time: 356 us; the launch traced here: 354 us
  waiting for transfers between devices  146 us (41%)
  local copies, waits for them, and re-layouts  63.8 us (18%)
  Pallas kernels  58.3 us (16%)
  matrix products  51.7 us (15%)
  between operations  16 us (4%)
  other arithmetic  13.4 us (4%)
  starting transfers between devices  3.95 us (1%)
    psum x1, waiting for transfers between devices, spread(): return lax.psum(jnp.where(mine, value, jnp.zeros_like(value)), axis)  132 us
    pallas_call x1, Pallas kernels, stack(): pl.pallas_call(functools.partial(stack_kernel, rows // band, band), grid=...  58.3 us
    dot_general x21, matrix products, add_row(): jnp.einsum('fhbc,fcd->fhbd', window, weights, precision=lax.Precision.HIG...  48.3 us
    dynamic_slice x21, local copies, waits for them, and re-layouts, add_row(): weights = lax.dynamic_index_in_dim(banded, offset, 1, keepdims=False)  29.3 us
    all_gather x1, waiting for transfers between devices, local(): whole = lax.all_gather(narrow, 'rows', axis=2, tiled=True)  13.8 us
    while x42, local copies, waits for them, and re-layouts  7.91 us
    slice x21, local copies, waits for them, and re-layouts, add_row(): leading = row_band[:, :, :columns].reshape(2, height, blocks, 128)  7.8 us
  transfers between devices with their start and end apart: 4, of which 2 were waited for; matrix products, arithmetic and copies ran while one was open for 2% of the time, Pallas kernels for 0%

profile of v1, /device:TPU:0, one launch (start us, length us, event | category | flops | bytes accessed | tf_op | source)
XLA Modules:
  0.0 354.4 jit_solution(18441195318511285640)
XLA Ops:
  6.5 1.5 fusion.16
  8.0 1.3 compare_and_fusion
  9.4 1.4 divide_select_fusion.1
  10.7 0.8 copy-done
  11.6 2.4 collective-permute-start
  14.0 1.3 collective-permute-start.1
  16.0 1.3 fusion.19
  19.7 3.4 fusion.10
  23.1 0.8 copy-done.1
  23.9 2.1 select_maximum_fusion
  26.0 94.3 %while.14 = (s32[]{:T(128)}, f32[2,32,32,128]{3,2,1,0:T(8,128)S(1)}, f32[2,52,4224]{2,1,0:T(8,128)S(1)}, f32[2,21,148,128]{3,1,2,0:T(8,128)}, s32[]{:T(128)}, /*index=5*/s32[]{:T(128)}, s32[]{}) while((s32[]{:T(128)}, f32[2,32,32,128]{3,2,1,0:T(8,128)S(1)}, f32[2,52,4224]{2,1,0:T(8,128)S(1)}, f32[2,21,148,128]{3,1,2,0:T(8,128)}, ...), condition=%wide.region_5.6_spmd.clone, body=%wide.region_4.5_spmd.clone.sunk | while | flops 466395136 | bytes 12152951 | solution.py:58
  26.0 1.4 constant_dynamic-slice_fusion.6
  28.2 2.3 fusion.24
  30.5 1.4 constant_dynamic-slice_fusion.6
  32.7 2.3 fusion.24
  35.0 1.4 constant_dynamic-slice_fusion.6
  37.2 2.3 fusion.24
  39.5 1.4 constant_dynamic-slice_fusion.6
  41.7 2.3 fusion.24
  44.0 1.4 constant_dynamic-slice_fusion.6
  46.2 2.3 fusion.24
  48.5 1.4 constant_dynamic-slice_fusion.6
  50.7 2.3 fusion.24
  53.0 1.4 constant_dynamic-slice_fusion.6
  55.1 2.3 fusion.24
  57.5 1.4 constant_dynamic-slice_fusion.6
  59.6 2.3 fusion.24
  62.0 1.4 constant_dynamic-slice_fusion.6
  64.1 2.3 fusion.24
  66.5 1.4 constant_dynamic-slice_fusion.6
  68.6 2.3 fusion.24
  70.9 1.4 constant_dynamic-slice_fusion.6
  73.1 2.3 fusion.24
  75.4 1.4 constant_dynamic-slice_fusion.6
  77.6 2.3 fusion.24
  79.9 1.4 constant_dynamic-slice_fusion.6
  82.1 2.3 fusion.24
  84.4 1.4 constant_dynamic-slice_fusion.6
  86.6 2.3 fusion.24
  88.9 1.4 constant_dynamic-slice_fusion.6
  91.1 2.3 fusion.24
  93.4 1.4 constant_dynamic-slice_fusion.6
  95.6 2.3 fusion.24
  97.9 1.4 constant_dynamic-slice_fusion.6
  100.1 2.3 fusion.24
  102.4 1.4 constant_dynamic-slice_fusion.6
  104.6 2.3 fusion.24
  106.9 1.4 constant_dynamic-slice_fusion.6
  109.1 2.3 fusion.24
  111.4 1.4 constant_dynamic-slice_fusion.6
  113.5 2.3 fusion.24
  115.9 1.4 constant_dynamic-slice_fusion.6
  118.0 2.3 fusion.24
  120.4 1.4 broadcast_select_fusion.1
  121.8 2.4 stack.31
  124.1 1.2 stack.33
  125.3 1.2 stack.32
  126.7 132.4 %all-reduce.4.cloned.1.call-done = (f32[1,2,32,4096]{3,2,1,0:T(8,128)}, f32[1,2,32,4096]{3,2,1,0:T(8,128)}, f32[1,2,32,4096]{3,2,1,0:T(8,128)}) async-done(((f32[1,2,32,4096]{3,2,1,0:T(8,128)}, f32[1,2,32,4096]{3,2,1,0:T(8,128)}, f32[1,2,32,4096]{3,2,1,0:T(8,128)}), (f32[1,2,32,4096]{3,2,1,0:T(8,128)}, f32[1,2,32,4096]{3,2,1,0:T(8,128)}, f32[1,2,32,4096]{3,2,1,0:T(8,128)})) %all-reduce.4.cloned.1.call-update) | async-done | bytes 3145744 | tf_op jit(solution)/shard_map/psum | solution.py:17
  259.2 3.8 %pad_maximum_fusion = f32[3,2,32,4096]{3,2,1,0:T(8,128)} fusion(f32[1,2,32,4096]{3,2,1,0:T(8,128)} %get-tuple-element.118, f32[1,2,32,4096]{3,2,1,0:T(8,128)} %get-tuple-element.119, f32[1,2,32,4096]{3,2,1,0:T(8,128)} %get-tuple-element.120), kind=kLoop, calls=%fused_computation.11 | loop fusion | flops 1572864 | bytes 6291456 | tf_op jit(solution)/shard_map/stack | solution.py:170
  263.8 0.7 reshape.76.shift_ref
  265.2 13.8 %all-gather.2.cloned.1.call-done = f32[3,2,64,4096]{3,2,1,0:T(8,128)} async-done(((f32[3,2,32,4096]{3,2,1,0:T(8,128)}), f32[3,2,64,4096]{3,2,1,0:T(8,128)}) %all-gather.2.cloned.1.call-update) | async-done | bytes 6291472 | tf_op jit(solution)/shard_map/all_gather | solution.py:171
  278.9 4.1 %copy.16 = f32[48,8,32,128]{3,2,1,0:T(8,128)S(1)} copy(f32[48,8,32,128]{3,1,2,0:T(8,128)} %bitcast.70) | data formatting | bytes 12582912
  283.0 6.3 %copy.20 = f32[6,64,32,128]{3,1,2,0:T(8,128)} copy(f32[6,64,32,128]{3,2,1,0:T(8,128)S(1)} %bitcast.68) | data formatting | bytes 12582912 | tf_op jit(solution)/shard_map/reshape | solution.py:173
  289.3 58.3 %stack.35 = f32[36,32,4096]{2,1,0:T(8,128)} custom-call(s32[216]{0:T(256)} %reshape.76.shift_ref, s32[1]{0:T(128)} %bitcast.where_ref, f32[1]{0:T(128)} %bitcast.1.floor_ref, f32[1,6,32,64,128]{4,3,2,1,0:T(8,128)} %bitcast.69), custom_call_target="tpu_custom_call" | custom-call | tf_op jit(solution)/shard_map/stack/pallas_call | solution.py:128
  (83 shorter events, 18.1 us)
Async XLA Ops:
  6.5 252.6 %all-reduce.4.cloned.1.call-start = ((), (), s32[]{:S(2)}) async-start(), calls=%async_computation.1 | async-start | bytes 6291456 | tf_op jit(solution)/shard_map/psum | solution.py:17
  9.3 6.0 %copy-start.2 = (f32[21,21]{1,0:T(8,128)S(1)}, f32[21,21]{1,0:T(8,128)}, u32[]{:S(2)}) copy-start(f32[21,21]{1,0:T(8,128)} %param.10) | copy-start | bytes 5296
  9.4 7.9 %copy-start.3 = (s32[3]{0:T(128)S(1)}, s32[3]{0:T(128)}, u32[]{:S(2)}) copy-start(s32[3]{0:T(128)} %param.12) | copy-start | bytes 40
  10.7 0.8 copy-start
  11.6 11.5 %collective-permute-start = (f32[2,10,4096]{2,1,0:T(8,128)S(1)}, f32[2,10,4096]{2,1,0:T(8,128)S(1)}, u32[]{:S(2)}, u32[]{:S(2)}) collective-permute-start(f32[2,10,4096]{2,1,0:T(8,128)S(1)} %get-tuple-element.126), channel_id=1, source_target_pairs={{0,1},{2,3},{4,5},{6,7},{8,9},{10,11},{12,13},{14,15},{16,17},{18,... | collective-permute-start | bytes 983048 | tf_op jit(solution)/shard_map/ppermute | solution.py:27
  14.0 9.9 %collective-permute-start.1 = (f32[2,10,4096]{2,1,0:T(8,128)S(1)}, f32[2,10,4096]{2,1,0:T(8,128)}, u32[]{:S(2)}, u32[]{:S(2)}) collective-permute-start(f32[2,10,4096]{2,1,0:T(8,128)S(1)} %get-tuple-element.127), channel_id=1, source_target_pairs={{1,0},{3,2},{5,4},{7,6},{9,8},{11,10},{13,12},{15,14},{17,16},{19,... | collective-permute-start | bytes 983048 | tf_op jit(solution)/shard_map/ppermute | solution.py:28
  23.1 0.8 copy-start.1
  126.5 152.4 %all-gather.2.cloned.1.call-start = ((), (), s32[]{:S(2)}) async-start(), calls=%async_computation | async-start | bytes 9437184 | tf_op jit(solution)/shard_map/all_gather | solution.py:171
  263.0 0.7 copy-start.4
Sparse Core Ops, SparseCore 0:
  126.6 132.4 all-reduce.3
  263.1 15.7 all-gather.1

commit v2 on v1

--- a/solution.py
+++ b/solution.py
@@ -12,51 +12,70 @@
 LANES = 128
 
 
-def spread(value, axis, root):
-    mine = lax.axis_index(axis) == root
-    return lax.psum(jnp.where(mine, value, jnp.zeros_like(value)), axis)
-
-
-def with_halo(value, sides, width):
-    for axis, dim in sides:
-        count, length = (lax.axis_size(axis), value.shape[dim])
-        up = [(i, (i + 1) % count) for i in range(count - 1)]
-        down = [(j, i) for i, j in up]
-        last = lax.slice_in_dim(value, length - width, length, axis=dim)
-        initial = lax.slice_in_dim(value, 0, width, axis=dim)
-        before = lax.ppermute(last, axis, up)
-        after = lax.ppermute(initial, axis, down)
-        value = jnp.concatenate([before, value, after], axis=dim)
-    return value
-
-
-def band_matrix(kernels, ksize):
-    inner = jnp.arange(128 + ksize - 1, dtype=jnp.int32)[:, None, None]
-    outer = jnp.arange(128, dtype=jnp.int32)[None, :, None]
-    offsets = jnp.arange(ksize, dtype=jnp.int32)[None, None, :]
-    onehot = (inner - outer == offsets).astype(jnp.float32)
-    return jnp.einsum("fkj,cdj->fkcd", kernels, onehot, precision=lax.Precision.HIGHEST)
-
-
-def correlate_pair(extended, banded, ksize):
+def split(value):
+    high = value.astype(jnp.bfloat16)
+    return high, (value - high.astype(jnp.float32)).astype(jnp.bfloat16)
+
+
+def correlate_kernel(ksize, owner_ref, taps_ref, pieces_ref, out_ref, acc, left):
+    bands, width, rows = pieces_ref.shape[1], pieces_ref.shape[2] - 1, pieces_ref.shape[3]
+    height = bands * rows
     half = ksize // 2
-    height = extended.shape[1] - (ksize - 1)
-    columns = extended.shape[2]
-    blocks = columns // 128
-    padded = jnp.pad(extended, ((0, 0), (0, 0), (half, 128 - half)))
-
-    def add_row(offset, summed):
-        row_band = lax.dynamic_slice_in_dim(padded, offset, height, 1)
-        leading = row_band[:, :, :columns].reshape(2, height, blocks, 128)
-        trailing = row_band[:, :, 128:].reshape(2, height, blocks, 128)[..., : ksize - 1]
-        window = jnp.concatenate([leading, trailing], axis=3)
-        weights = lax.dynamic_index_in_dim(banded, offset, 1, keepdims=False)
-        return summed + jnp.einsum(
-            "fhbc,fcd->fhbd", window, weights, precision=lax.Precision.HIGHEST
-        )
-
-    summed = lax.fori_loop(0, ksize, add_row, jnp.zeros((2, height, blocks, 128), jnp.float32))
-    return summed.reshape(2, height, columns)
+    window = 2 * LANES
+    lane = lax.broadcasted_iota(jnp.int32, (rows, LANES), 1)
+    low = lane < LANES // 2
+    for e in range(EPOCHS):
+        slot = owner_ref[e]
+        for r in range(bands):
+            blocks = [pieces_ref[slot, r, b] for b in range(width + 1)]
+            for b in range(width):
+                after = blocks[b + 1]
+                before = blocks[b - 1] if b else blocks[width]
+                place = pl.ds((e * width + b) * height + r * rows, rows)
+                own_high, own_low = split(blocks[b])
+                side_high, side_low = split(jnp.where(low, after, before))
+                left[place, 0:LANES] = own_high
+                left[place, LANES:window] = side_high
+                left[place, window : window + LANES] = own_low
+                left[place, window + LANES : 2 * window] = side_low
+    acc[...] = jnp.zeros_like(acc)
+
+    def band(a):
+        row = jnp.broadcast_to(taps_ref[a : a + 1, :], (window, window))
+        return pltpu.roll(row, 0, 1, stride=1, stride_axis=0)[:, :LANES]
+
+    for a in range(0, ksize, 2):
+        count = min(2, ksize - a)
+        weights = jnp.concatenate([band(a + i) for i in range(count)], axis=1)
+        high, small = split(weights)
+        for e in range(EPOCHS):
+            place = pl.ds(e * width * height, width * height)
+            values = left[place, :]
+            product = jnp.dot(values[:, :window], high, preferred_element_type=jnp.float32)
+            product += jnp.dot(values[:, window:], high, preferred_element_type=jnp.float32)
+            product += jnp.dot(values[:, :window], small, preferred_element_type=jnp.float32)
+            for i in range(count):
+                shift = ksize - 1 - (a + i)
+                part = product[:, i * LANES : (i + 1) * LANES].reshape(width, height, LANES)
+                acc[e, :, shift : shift + height, :] += part
+    out_ref[...] = acc[:, :, half : half + height, :]
+
+
+def correlate(pieces, taps, epoch_owner, ksize):
+    bands, width, rows = pieces.shape[1], pieces.shape[2] - 1, pieces.shape[3]
+    height = bands * rows
+    vmem = pl.BlockSpec(memory_space=pltpu.VMEM)
+    return pl.pallas_call(
+        functools.partial(correlate_kernel, ksize),
+        out_shape=jax.ShapeDtypeStruct((EPOCHS, width, height, LANES), jnp.float32),
+        in_specs=[pl.BlockSpec(memory_space=pltpu.SMEM), vmem, vmem],
+        out_specs=vmem,
+        scratch_shapes=[
+            pltpu.VMEM((EPOCHS, width, height + ksize - 1, LANES), jnp.float32),
+            pltpu.VMEM((EPOCHS * width * height, 4 * LANES), jnp.bfloat16),
+        ],
+        name="correlate",
+    )(epoch_owner, taps, pieces)
 
 
 def stack_kernel(bands, band, shift_ref, where_ref, floor_ref, planes_ref, out_ref, held, sem):
@@ -101,7 +120,7 @@
 
     def rolled(e, f, b):
         row, start, amount, _ = places[e]
-        return pltpu.roll(held[2 * e + f, start + b, pl.ds(row, band), :], amount, 1)
+        return pltpu.roll(held[f * EPOCHS + e, start + b, pl.ds(row, band), :], amount, 1)
 
     def step(b, before):
         sums = [None, None]
@@ -144,16 +163,29 @@
     )
 
 
+def cut(plane, pieces):
+    rows, columns = plane.shape
+    blocks = columns // LANES
+    tiles = plane.reshape(rows, blocks, LANES).transpose(1, 0, 2)
+    own = tiles.reshape(pieces, blocks // pieces, rows, LANES)
+    none = jnp.zeros((1, rows, LANES), jnp.float32)
+    after = jnp.concatenate([own[1:, 0], none])
+    before = jnp.concatenate([none, own[:-1, -1]])
+    lane = jnp.arange(LANES, dtype=jnp.int32)
+    sides = jnp.where(lane < LANES // 2, after, before)
+    return jnp.concatenate([own, sides[:, None]], axis=1)
+
+
 def local(images, variance, spread_kernel, shifts, epoch_owner, valid_rows):
     exposure = images[0]
     noise_var = variance[0]
     band_rows = exposure.shape[0]
-    columns = exposure.shape[1]
     ksize = spread_kernel.shape[0]
     half = ksize // 2
     kernel_norm = spread_kernel / jnp.sum(spread_kernel)
     kernel_sq = kernel_norm * kernel_norm
     floor = 0.5 * jnp.sum(kernel_sq)
+    slots = lax.axis_size("vel")
     vel_index = lax.axis_index("vel")
     row_index = lax.axis_index("rows")
     owned = epoch_owner == vel_index
@@ -163,15 +195,16 @@
     usable = (row_ids >= lower_row) & (row_ids < upper_row)
     weighted = jnp.where(usable, exposure / noise_var, jnp.float32(0.0))
     inverse = jnp.where(usable, 1.0 / noise_var, jnp.float32(0.0))
-    fields_pair = jnp.stack([weighted, inverse])
-    extended = with_halo(fields_pair, (("rows", 1),), half)
-    banded = band_matrix(jnp.stack([kernel_norm, kernel_sq]), ksize)
-    correlated = correlate_pair(extended, banded, ksize)
-    narrow = jnp.stack([spread(correlated, "vel", epoch_owner[epoch]) for epoch in range(EPOCHS)])
-    whole = lax.all_gather(narrow, "rows", axis=2, tiled=True)
-    rows = whole.shape[2]
-    planes = whole.reshape(2 * EPOCHS, rows, columns // LANES, LANES).transpose(0, 2, 1, 3)
-    return stack(planes[None], shifts, floor, band_rows, row_index)
+    sent = jnp.stack([cut(weighted, slots), cut(inverse, slots)], axis=1)
+    sent = sent.reshape((-1,) + sent.shape[2:])
+    got = lax.all_to_all(sent, ("vel", "rows"), 0, 0, tiled=True)
+    got = got.reshape((slots, 2) + got.shape[1:])
+    kernel = jnp.where(row_index == 0, kernel_norm, kernel_sq)
+    taps = jnp.roll(jnp.pad(kernel[:, ::-1], ((0, 0), (0, 2 * LANES - ksize))), -half, axis=1)
+    mine = correlate(got, taps, epoch_owner, ksize)
+    planes = lax.all_gather(mine, ("vel", "rows"), axis=0)
+    planes = planes.reshape((slots, 2 * EPOCHS) + planes.shape[2:])
+    return stack(planes, shifts, floor, band_rows, row_index)
 
 
 def solution(mesh):

time: 356 us -> 186 us (0.52)
  local copies, waits for them, and re-layouts: 63.8 us -> 3.87 us
  waiting for transfers between devices: 146 us -> 87.8 us
  matrix products: 51.7 us -> 0 us
  Pallas kernels: 58.3 us -> 65 us
  other arithmetic: 13.4 us -> 7.1 us
  starting transfers between devices: 3.95 us -> 7.59 us
    psum x1 -> x0, waiting for transfers between devices: 132 us -> none  [spread(): return lax.psum(jnp.where(mine, value, jnp.zeros_like(value)), axis)]
    dot_general x22 -> x0, matrix products: 51.7 us -> none  [the longest x21 48.3 us: add_row(): jnp.einsum('fhbc,fcd->fhbd', window, weights, precision=lax.Precision.HIG...]
    all_gather x1, waiting for transfers between devices: 13.8 us -> 63.4 us  [local(): planes = lax.all_gather(mine, ('vel', 'rows'), axis=0)]
    dynamic_slice x21 -> x0, local copies, waits for them, and re-layouts: 29.3 us -> none  [add_row(): weights = lax.dynamic_index_in_dim(banded, offset, 1, keepdims=False)]
    all_to_all x0 -> x1, waiting for transfers between devices: none -> 24.4 us  [local(): got = lax.all_to_all(sent, ('vel', 'rows'), 0, 0, tiled=True)]
    while x42 -> x0, local copies, waits for them, and re-layouts: 7.91 us -> none
    slice x22 -> x5, local copies, waits for them, and re-layouts: 8.42 us -> 0.55 us  [the longest x2 0.33 us: cut(): after = jnp.concatenate([own[1:, 0], none])]
    all_to_all x0 -> x1, starting transfers between devices: none -> 7.55 us  [local(): got = lax.all_to_all(sent, ('vel', 'rows'), 0, 0, tiled=True)]
  transfers between devices with their start and end apart: 4 -> 2, of which waited for: 2 -> 2; matrix products, arithmetic and copies ran while one was open for 2% -> 2% of each run, Pallas kernels for 0% -> 0%
where the time goes in v2:
time: 186 us
  waiting for transfers between devices  87.8 us (47%)
  Pallas kernels  65 us (35%)
  between operations  14.2 us (8%)
  starting transfers between devices  7.59 us (4%)
  other arithmetic  7.1 us (4%)
  local copies, waits for them, and re-layouts  3.87 us (2%)
    all_gather x1, waiting for transfers between devices, local(): planes = lax.all_gather(mine, ('vel', 'rows'), axis=0)  63.4 us
    pallas_call x1, Pallas kernels, stack(): pl.pallas_call(functools.partial(stack_kernel, rows // band, band), grid=...  58.3 us
    all_to_all x1, waiting for transfers between devices, local(): got = lax.all_to_all(sent, ('vel', 'rows'), 0, 0, tiled=True)  24.4 us
    all_to_all x1, starting transfers between devices, local(): got = lax.all_to_all(sent, ('vel', 'rows'), 0, 0, tiled=True)  7.55 us
    pallas_call x1, Pallas kernels, correlate(): pl.pallas_call(functools.partial(correlate_kernel, ksize), out_shape=jax....  6.64 us
  transfers between devices with their start and end apart: 2, of which 2 were waited for; matrix products, arithmetic and copies ran while one was open for 2% of the time, Pallas kernels for 0%

profile of v2, /device:TPU:0, one launch (start us, length us, event | category | flops | bytes accessed | tf_op | source)
XLA Modules:
  0.0 185.6 jit_solution(12564758751140985754)
XLA Ops:
  6.5 1.3 divide_bitcast_fusion.1
  7.8 0.0 copy-start.3
  7.8 0.0 copy-start.4
  7.8 0.1 copy.34
  7.9 0.1 copy.35
  8.1 0.4 copy-done.3
  8.5 0.0 copy-done.4
  8.5 0.6 fusion
  9.1 1.2 compare_and_fusion
  10.4 0.1 bitcast_select_fusion.1
  10.5 0.2 fusion.3
  10.7 0.3 copy.29
  11.0 0.2 fusion.2
  11.2 0.3 copy.25
  11.6 0.1 maximum_bitcast_fusion
  11.6 0.1 maximum_bitcast_fusion.1
  11.7 1.2 pad_maximum_fusion
  12.9 0.0 copy-start.1
  12.9 7.5 %all-to-all-start = ((f32[16,5,32,128]{3,2,1,0:T(8,128)}), f32[16,5,32,128]{3,2,1,0:T(8,128)S(1)}, u32[]{:S(2)}, u32[]{:S(2)}) async-start(f32[16,5,32,128]{3,2,1,0:T(8,128)} %bitcast.19), calls=%async_computation | async-start | bytes 2621440 | tf_op jit(solution)/shard_map/all_to_all | solution.py:200
  20.5 0.0 copy-start.2
  20.5 0.0 all-gather.3.cloned.1.call-start
  20.5 0.0 copy-done.1
  20.5 0.6 reduce_sum.36
  21.1 1.2 multiply_select_fusion
  22.4 0.1 slice.39
  22.4 0.1 rev.3
  22.5 0.1 slice.32
  22.6 0.1 pad_slice_fusion
  22.6 0.7 pad_maximum_fusion.1.taps_ref
  23.3 24.4 %all-to-all-done = f32[16,5,32,128]{3,2,1,0:T(8,128)S(1)} async-done(((f32[16,5,32,128]{3,2,1,0:T(8,128)}), f32[16,5,32,128]{3,2,1,0:T(8,128)S(1)}, u32[]{:S(2)}, u32[]{:S(2)}) %all-to-all-start) | async-done | bytes 1310752 | tf_op jit(solution)/shard_map/all_to_all | solution.py:200
  47.7 0.0 copy-start
  47.7 1.1 copy-done
  48.8 6.6 %correlate.1 = f32[3,4,64,128]{3,2,1,0:T(8,128)} custom-call(s32[3]{0:T(128)} %owner_ref.1, f32[21,256]{1,0:T(8,128)} %pad_maximum_fusion.1.taps_ref, f32[8,2,5,32,128]{4,3,2,1,0:T(8,128)} %bitcast.44), custom_call_target="tpu_custom_call" | custom-call | tf_op jit(solution)/shard_map/correlate/pallas_call | solution.py:68
  55.4 0.0 all-gather.3.cloned.1.call-update
  55.5 0.0 copy-done.2
  55.5 0.1 copy.22
  55.6 0.7 reshape.53.shift_ref
  57.0 63.4 %all-gather.3.cloned.1.call-done = f32[48,4,64,128]{3,2,1,0:T(8,128)} async-done(((f32[3,4,64,128]{3,2,1,0:T(8,128)}), f32[48,4,64,128]{3,2,1,0:T(8,128)}) %all-gather.3.cloned.1.call-update) | async-done | bytes 6291472 | tf_op jit(solution)/shard_map/all_gather | solution.py:205
  120.4 58.3 %stack.13 = f32[36,32,4096]{2,1,0:T(8,128)} custom-call(s32[216]{0:T(256)} %reshape.53.shift_ref, s32[1]{0:T(128)} %bitcast.where_ref, f32[1]{0:T(128)} %bitcast.1.floor_ref, f32[8,6,4,64,128]{4,3,2,1,0:T(8,128)} %bitcast.43), custom_call_target="tpu_custom_call" | custom-call | tf_op jit(solution)/shard_map/stack/pallas_call | solution.py:147
  (4 shorter events, 0.1 us)
Async XLA Ops:
  7.8 0.7 copy-start.3
  7.8 0.7 copy-start.4
  12.9 7.6 %copy-start.1 = (f32[21,21]{1,0:T(8,128)S(1)}, f32[21,21]{1,0:T(8,128)}, u32[]{:S(2)}) copy-start(f32[21,21]{1,0:T(8,128)} %param.8) | copy-start | bytes 5296
  12.9 34.8 %all-to-all-start = ((f32[16,5,32,128]{3,2,1,0:T(8,128)}), f32[16,5,32,128]{3,2,1,0:T(8,128)S(1)}, u32[]{:S(2)}, u32[]{:S(2)}) async-start(f32[16,5,32,128]{3,2,1,0:T(8,128)} %bitcast.19), calls=%async_computation | async-start | bytes 2621440 | tf_op jit(solution)/shard_map/all_to_all | solution.py:200
  20.5 35.0 %copy-start.2 = (s32[36,3,2]{0,2,1:T(2,128)S(1)}, s32[36,3,2]{0,2,1:T(2,128)}, u32[]{:S(2)}) copy-start(s32[36,3,2]{0,2,1:T(2,128)} %param.9) | copy-start | bytes 2596
  20.5 99.9 %all-gather.3.cloned.1.call-start = ((), (), s32[]{:S(2)}) async-start(), calls=%async_computation.1 | async-start | bytes 6684672 | tf_op jit(solution)/shard_map/all_gather | solution.py:205
  47.7 1.1 copy-start
Sparse Core Ops, SparseCore 0:
  55.6 64.7 all-gather.2

commit v3 on v2

--- a/solution.py
+++ b/solution.py
@@ -76,6 +76,87 @@
         ],
         name="correlate",
     )(epoch_owner, taps, pieces)
+
+
+MESH = pl.DeviceIdType.MESH
+
+
+def ring_kernel(count, mine_ref, out_ref, own_sem, send_sem, recv_sem, pass_sem, take_sem):
+    me, core = lax.axis_index("vel"), lax.axis_index("rows")
+    other = 1 - core
+    half = mine_ref.shape[1] // 2
+
+    def index_at(position):
+        position = (position + count) % count
+        late = position // (count // 2)
+        return (1 - late) * (2 * position) + late * (2 * (count - 1 - position) + 1)
+
+    odd = me % 2
+    position = (1 - odd) * (me // 2) + odd * (count - 1 - me // 2)
+    ahead = [index_at(position + 1), index_at(position - 1)]
+
+    barrier = pltpu.get_barrier_semaphore()
+    for target in ({"vel": ahead[0]}, {"vel": ahead[1]}, {"rows": other}):
+        pl.semaphore_signal(barrier, inc=1, device_id=target, device_id_type=MESH)
+    pl.semaphore_wait(barrier, 3)
+
+    own = pltpu.make_async_copy(mine_ref, out_ref.at[me, core], own_sem)
+    own.start()
+    sent, passed = {}, {}
+    for s in range(count):
+        for e in range(EPOCHS):
+            for d in range(2):
+                owner = index_at(position - s) if d == 0 else index_at(position + s)
+                part = pl.ds(d * half, half)
+                place = out_ref.at[owner, core, e, part]
+                if s:
+                    sent[s - 1, e, d].wait_recv()
+                source = place if s else mine_ref.at[e, part]
+                if s < count - 1:
+                    copy = pltpu.make_async_remote_copy(
+                        src_ref=source,
+                        dst_ref=place,
+                        send_sem=send_sem.at[s, e, d],
+                        recv_sem=recv_sem.at[s, e, d],
+                        device_id={"vel": ahead[d]},
+                        device_id_type=MESH,
+                    )
+                    copy.start()
+                    sent[s, e, d] = copy
+                copy = pltpu.make_async_remote_copy(
+                    src_ref=source,
+                    dst_ref=place,
+                    send_sem=pass_sem.at[s, e, d],
+                    recv_sem=take_sem.at[s, e, d],
+                    device_id={"rows": other},
+                    device_id_type=MESH,
+                )
+                copy.start()
+                passed[s, e, d] = copy
+    for copy in sent.values():
+        copy.wait_send()
+    for copy in passed.values():
+        copy.wait()
+    own.wait()
+
+
+def gather(mine):
+    count = lax.axis_size("vel")
+    return pl.pallas_call(
+        functools.partial(ring_kernel, count),
+        out_shape=jax.ShapeDtypeStruct((count, 2) + mine.shape, jnp.float32),
+        in_specs=[pl.BlockSpec(memory_space=pltpu.VMEM)],
+        out_specs=pl.BlockSpec(memory_space=pl.ANY),
+        scratch_shapes=[
+            pltpu.SemaphoreType.DMA,
+            pltpu.SemaphoreType.DMA((count - 1, EPOCHS, 2)),
+            pltpu.SemaphoreType.DMA((count - 1, EPOCHS, 2)),
+            pltpu.SemaphoreType.DMA((count, EPOCHS, 2)),
+            pltpu.SemaphoreType.DMA((count, EPOCHS, 2)),
+        ],
+        compiler_params=pltpu.CompilerParams(collective_id=0, has_side_effects=True),
+        name="gather",
+    )(mine)
 
 
 def stack_kernel(bands, band, shift_ref, where_ref, floor_ref, planes_ref, out_ref, held, sem):
@@ -202,8 +283,8 @@
     kernel = jnp.where(row_index == 0, kernel_norm, kernel_sq)
     taps = jnp.roll(jnp.pad(kernel[:, ::-1], ((0, 0), (0, 2 * LANES - ksize))), -half, axis=1)
     mine = correlate(got, taps, epoch_owner, ksize)
-    planes = lax.all_gather(mine, ("vel", "rows"), axis=0)
-    planes = planes.reshape((slots, 2 * EPOCHS) + planes.shape[2:])
+    planes = gather(mine)
+    planes = planes.reshape((slots, 2 * EPOCHS) + planes.shape[3:])
     return stack(planes, shifts, floor, band_rows, row_index)
 
 

time: 186 us -> 149 us (0.80)
  waiting for transfers between devices: 87.8 us -> 23 us
  Pallas kernels: 65 us -> 106 us
  between operations: 14.2 us -> 0.78 us
    all_gather x1 -> x0, waiting for transfers between devices: 63.4 us -> none  [local(): planes = lax.all_gather(mine, ('vel', 'rows'), axis=0)]
    pallas_call x0 -> x1, Pallas kernels: none -> 41.5 us  [gather(): pl.pallas_call(functools.partial(ring_kernel, count), out_shape=jax.Shape...]
  transfers between devices with their start and end apart: 2 -> 1, of which waited for: 2 -> 1; matrix products, arithmetic and copies ran while one was open for 2% -> 2% of each run, Pallas kernels for 0% -> 0%
where the time goes in v3:
time: 149 us
  Pallas kernels  106 us (71%)
  waiting for transfers between devices  23 us (15%)
  starting transfers between devices  7.55 us (5%)
  other arithmetic  7.12 us (5%)
  local copies, waits for them, and re-layouts  3.86 us (3%)
    pallas_call x1, Pallas kernels, stack(): pl.pallas_call(functools.partial(stack_kernel, rows // band, band), grid=...  58.4 us
    pallas_call x1, Pallas kernels, gather(): pl.pallas_call(functools.partial(ring_kernel, count), out_shape=jax.Shape...  41.5 us
    all_to_all x1, waiting for transfers between devices, local(): got = lax.all_to_all(sent, ('vel', 'rows'), 0, 0, tiled=True)  23 us
    all_to_all x1, starting transfers between devices, local(): got = lax.all_to_all(sent, ('vel', 'rows'), 0, 0, tiled=True)  7.55 us
    pallas_call x1, Pallas kernels, correlate(): pl.pallas_call(functools.partial(correlate_kernel, ksize), out_shape=jax....  6.65 us
  transfers between devices with their start and end apart: 1, of which 1 were waited for; matrix products, arithmetic and copies ran while one was open for 2% of the time, Pallas kernels for 0%

profile of v3, /device:TPU:0, one launch (start us, length us, event | category | flops | bytes accessed | tf_op | source)
XLA Modules:
  0.0 148.8 jit_solution(8957919970974247569)
XLA Ops:
  0.0 1.3 divide_bitcast_fusion.1
  1.3 0.0 copy-start.3
  1.3 0.0 copy-start.4
  1.3 0.1 copy.26
  1.4 0.1 copy.27
  1.5 0.4 copy-done.3
  1.9 0.0 copy-done.4
  2.0 0.6 fusion
  2.6 1.3 compare_and_fusion
  3.9 0.1 bitcast_select_fusion.1
  4.0 0.2 fusion.3
  4.2 0.3 copy.21
  4.5 0.2 fusion.2
  4.7 0.3 copy.17
  5.1 0.1 maximum_bitcast_fusion
  5.2 0.1 maximum_bitcast_fusion.1
  5.2 1.2 pad_maximum_fusion
  6.4 0.0 copy-start.1
  6.4 0.0 copy-start.2
  6.4 7.5 %all-to-all-start = ((f32[16,5,32,128]{3,2,1,0:T(8,128)}), f32[16,5,32,128]{3,2,1,0:T(8,128)S(1)}, u32[]{:S(2)}, u32[]{:S(2)}) async-start(f32[16,5,32,128]{3,2,1,0:T(8,128)} %bitcast.19), calls=%async_computation | async-start | bytes 2621440 | tf_op jit(solution)/shard_map/all_to_all | solution.py:281
  14.0 0.0 copy-done.1
  14.0 0.6 reduce_sum.36
  14.6 1.2 multiply_select_fusion
  15.8 0.1 slice.39
  15.9 0.1 rev.3
  15.9 0.1 slice.32
  16.0 0.0 copy-done.2
  16.0 0.1 copy.14
  16.1 0.7 reshape.53.shift_ref
  17.5 0.1 pad_slice_fusion
  17.6 0.7 pad_maximum_fusion.1.taps_ref
  18.2 23.0 %all-to-all-done = f32[16,5,32,128]{3,2,1,0:T(8,128)S(1)} async-done(((f32[16,5,32,128]{3,2,1,0:T(8,128)}), f32[16,5,32,128]{3,2,1,0:T(8,128)S(1)}, u32[]{:S(2)}, u32[]{:S(2)}) %all-to-all-start) | async-done | bytes 1310752 | tf_op jit(solution)/shard_map/all_to_all | solution.py:281
  41.3 0.0 copy-start
  41.3 1.1 copy-done
  42.3 6.7 %correlate.1.mine_ref = f32[3,4,64,128]{3,2,1,0:T(8,128)} custom-call(s32[3]{0:T(128)} %owner_ref.1, f32[21,256]{1,0:T(8,128)} %pad_maximum_fusion.1.taps_ref, f32[8,2,5,32,128]{4,3,2,1,0:T(8,128)} %bitcast.44), custom_call_target="tpu_custom_call" | custom-call | tf_op jit(solution)/shard_map/correlate/pallas_call | solution.py:68
  49.0 41.5 %gather.1 = f32[8,2,3,4,64,128]{5,4,3,2,1,0:T(8,128)} custom-call(f32[3,4,64,128]{3,2,1,0:T(8,128)} %correlate.1.mine_ref), custom_call_target="tpu_custom_call" | custom-call | tf_op jit(solution)/shard_map/gather/pallas_call | solution.py:145
  90.5 58.4 %stack.13 = f32[36,32,4096]{2,1,0:T(8,128)} custom-call(s32[216]{0:T(256)} %reshape.53.shift_ref, s32[1]{0:T(128)} %bitcast.where_ref, f32[1]{0:T(128)} %bitcast.1.floor_ref, f32[8,6,4,64,128]{4,3,2,1,0:T(8,128)} %bitcast.43), custom_call_target="tpu_custom_call" | custom-call | tf_op jit(solution)/shard_map/stack/pallas_call | solution.py:228
  (4 shorter events, 0.1 us)
Async XLA Ops:
  1.3 0.7 copy-start.3
  1.3 0.7 copy-start.4
  6.4 7.6 %copy-start.1 = (f32[21,21]{1,0:T(8,128)S(1)}, f32[21,21]{1,0:T(8,128)}, u32[]{:S(2)}) copy-start(f32[21,21]{1,0:T(8,128)} %param.8) | copy-start | bytes 5296
  6.4 9.6 %copy-start.2 = (s32[36,3,2]{0,2,1:T(2,128)S(1)}, s32[36,3,2]{0,2,1:T(2,128)}, u32[]{:S(2)}) copy-start(s32[36,3,2]{0,2,1:T(2,128)} %param.9) | copy-start | bytes 2596
  6.4 34.8 %all-to-all-start = ((f32[16,5,32,128]{3,2,1,0:T(8,128)}), f32[16,5,32,128]{3,2,1,0:T(8,128)S(1)}, u32[]{:S(2)}, u32[]{:S(2)}) async-start(f32[16,5,32,128]{3,2,1,0:T(8,128)} %bitcast.19), calls=%async_computation | async-start | bytes 2621440 | tf_op jit(solution)/shard_map/all_to_all | solution.py:281
  41.3 1.1 copy-start

commit v4 on v3

--- a/solution.py
+++ b/solution.py
@@ -217,7 +217,7 @@
         return tuple(after)
 
     initial = tuple(rolled(e, f, 0) for e in range(EPOCHS) for f in range(2))
-    lax.fori_loop(0, blocks, step, initial, unroll=4)
+    lax.fori_loop(0, blocks, step, initial, unroll=blocks)
 
 
 def stack(planes, shifts, floor, band, row_index):

time: 149 us -> 129 us (0.87)
  Pallas kernels: 106 us -> 86.3 us
    pallas_call x1, Pallas kernels: 58.4 us -> 38.2 us  [stack(): pl.pallas_call(functools.partial(stack_kernel, rows // band, band), grid=...]
  transfers between devices with their start and end apart: 1 -> 1, of which waited for: 1 -> 1; matrix products, arithmetic and copies ran while one was open for 2% -> 3% of each run, Pallas kernels for 0% -> 0%
where the time goes in v4:
time: 129 us
  Pallas kernels  86.3 us (67%)
  waiting for transfers between devices  23 us (18%)
  starting transfers between devices  7.55 us (6%)
  other arithmetic  7.12 us (6%)
  local copies, waits for them, and re-layouts  3.86 us (3%)
    pallas_call x1, Pallas kernels, gather(): pl.pallas_call(functools.partial(ring_kernel, count), out_shape=jax.Shape...  41.5 us
    pallas_call x1, Pallas kernels, stack(): pl.pallas_call(functools.partial(stack_kernel, rows // band, band), grid=...  38.2 us
    all_to_all x1, waiting for transfers between devices, local(): got = lax.all_to_all(sent, ('vel', 'rows'), 0, 0, tiled=True)  23 us
    all_to_all x1, starting transfers between devices, local(): got = lax.all_to_all(sent, ('vel', 'rows'), 0, 0, tiled=True)  7.55 us
    pallas_call x1, Pallas kernels, correlate(): pl.pallas_call(functools.partial(correlate_kernel, ksize), out_shape=jax....  6.65 us
  transfers between devices with their start and end apart: 1, of which 1 were waited for; matrix products, arithmetic and copies ran while one was open for 3% of the time, Pallas kernels for 0%

profile of v4, /device:TPU:0, one launch (start us, length us, event | category | flops | bytes accessed | tf_op | source)
XLA Modules:
  0.0 128.6 jit_solution(869108106490337290)
XLA Ops:
  0.0 1.3 divide_bitcast_fusion.1
  1.3 0.0 copy-start.3
  1.3 0.0 copy-start.4
  1.3 0.1 copy.26
  1.4 0.1 copy.27
  1.5 0.4 copy-done.3
  1.9 0.0 copy-done.4
  2.0 0.6 fusion
  2.6 1.3 compare_and_fusion
  3.9 0.1 bitcast_select_fusion.1
  4.0 0.2 fusion.3
  4.2 0.3 copy.21
  4.5 0.2 fusion.2
  4.7 0.3 copy.17
  5.1 0.1 maximum_bitcast_fusion
  5.2 0.1 maximum_bitcast_fusion.1
  5.2 1.2 pad_maximum_fusion
  6.4 0.0 copy-start.1
  6.4 0.0 copy-start.2
  6.4 7.5 %all-to-all-start = ((f32[16,5,32,128]{3,2,1,0:T(8,128)}), f32[16,5,32,128]{3,2,1,0:T(8,128)S(1)}, u32[]{:S(2)}, u32[]{:S(2)}) async-start(f32[16,5,32,128]{3,2,1,0:T(8,128)} %bitcast.19), calls=%async_computation | async-start | bytes 2621440 | tf_op jit(solution)/shard_map/all_to_all | solution.py:281
  14.0 0.0 copy-done.1
  14.0 0.6 reduce_sum.36
  14.6 1.2 multiply_select_fusion
  15.8 0.1 slice.39
  15.9 0.1 rev.3
  15.9 0.1 slice.32
  16.0 0.0 copy-done.2
  16.0 0.1 copy.14
  16.1 0.7 reshape.53.shift_ref
  17.5 0.1 pad_slice_fusion
  17.6 0.7 pad_maximum_fusion.1.taps_ref
  18.2 23.0 %all-to-all-done = f32[16,5,32,128]{3,2,1,0:T(8,128)S(1)} async-done(((f32[16,5,32,128]{3,2,1,0:T(8,128)}), f32[16,5,32,128]{3,2,1,0:T(8,128)S(1)}, u32[]{:S(2)}, u32[]{:S(2)}) %all-to-all-start) | async-done | bytes 1310752 | tf_op jit(solution)/shard_map/all_to_all | solution.py:281
  41.3 0.0 copy-start
  41.3 1.1 copy-done
  42.3 6.7 %correlate.1.mine_ref = f32[3,4,64,128]{3,2,1,0:T(8,128)} custom-call(s32[3]{0:T(128)} %owner_ref.1, f32[21,256]{1,0:T(8,128)} %pad_maximum_fusion.1.taps_ref, f32[8,2,5,32,128]{4,3,2,1,0:T(8,128)} %bitcast.44), custom_call_target="tpu_custom_call" | custom-call | tf_op jit(solution)/shard_map/correlate/pallas_call | solution.py:68
  49.0 41.5 %gather.1 = f32[8,2,3,4,64,128]{5,4,3,2,1,0:T(8,128)} custom-call(f32[3,4,64,128]{3,2,1,0:T(8,128)} %correlate.1.mine_ref), custom_call_target="tpu_custom_call" | custom-call | tf_op jit(solution)/shard_map/gather/pallas_call | solution.py:145
  90.5 38.2 %stack.13 = f32[36,32,4096]{2,1,0:T(8,128)} custom-call(s32[216]{0:T(256)} %reshape.53.shift_ref, s32[1]{0:T(128)} %bitcast.where_ref, f32[1]{0:T(128)} %bitcast.1.floor_ref, f32[8,6,4,64,128]{4,3,2,1,0:T(8,128)} %bitcast.43), custom_call_target="tpu_custom_call" | custom-call | tf_op jit(solution)/shard_map/stack/pallas_call | solution.py:228
  (4 shorter events, 0.1 us)
Async XLA Ops:
  1.3 0.7 copy-start.3
  1.3 0.7 copy-start.4
  6.4 7.6 %copy-start.1 = (f32[21,21]{1,0:T(8,128)S(1)}, f32[21,21]{1,0:T(8,128)}, u32[]{:S(2)}) copy-start(f32[21,21]{1,0:T(8,128)} %param.8) | copy-start | bytes 5296
  6.4 9.6 %copy-start.2 = (s32[36,3,2]{0,2,1:T(2,128)S(1)}, s32[36,3,2]{0,2,1:T(2,128)}, u32[]{:S(2)}) copy-start(s32[36,3,2]{0,2,1:T(2,128)} %param.9) | copy-start | bytes 2596
  6.4 34.8 %all-to-all-start = ((f32[16,5,32,128]{3,2,1,0:T(8,128)}), f32[16,5,32,128]{3,2,1,0:T(8,128)S(1)}, u32[]{:S(2)}, u32[]{:S(2)}) async-start(f32[16,5,32,128]{3,2,1,0:T(8,128)} %bitcast.19), calls=%async_computation | async-start | bytes 2621440 | tf_op jit(solution)/shard_map/all_to_all | solution.py:281
  41.3 1.1 copy-start
